TPU v7x, 32 devices: a whole 2x2x4 slice. The times are simulated.
32 devices in a mesh: dp: 8 (over z, y), tensor: 4 (over x, core).
Axes of the slice: x: 2, y: 2, z: 4, core: 2. Of those that a mesh axis runs over, the one named last changes fastest.
Arguments:
- hidden: bfloat16 [12288, 1536], P('dp'), may hold values from -6 to 6
- segment_ids: int32 [12288], P('dp'), may hold values from -1 to 12287, as said below
- norm_gain: float32 [1536], replicated, may hold values from 0.5 to 1.5
- gate_weight: bfloat16 [1536, 3072], P(None, 'tensor'), may hold values from -0.15625 to 0.15625
- input_weight: bfloat16 [1536, 3072], P(None, 'tensor'), may hold values from -0.15625 to 0.15625
- step_weight: bfloat16 [1536, 48], P(None, 'tensor'), may hold values from -0.15625 to 0.15625
- state_weight: bfloat16 [1536, 256], replicated, may hold values from -0.15625 to 0.15625
- conv_weight: float32 [4, 3072], P(None, 'tensor'), may hold values from -3 to 3
- state_conv_weight: float32 [4, 256], replicated, may hold values from -3 to 3
- conv_bias: float32 [3072], P('tensor'), may hold values from -0.5 to 0.5
- state_conv_bias: float32 [256], replicated, may hold values from -0.5 to 0.5
- step_bias: float32 [48], P('tensor'), may hold values from -6.9 to -2.25
- decay_log: float32 [48], P('tensor'), may hold values from 0 to 2.77
- skip_gain: float32 [48], P('tensor'), may hold values from 0.5 to 1.5
- gate_norm_gain: float32 [3072], P('tensor'), may hold values from 0.5 to 1.5
- out_weight: bfloat16 [3072, 1536], P('tensor'), may hold values from -0.109375 to 0.109375
- cotangent: bfloat16 [12288, 1536], P('dp'), may hold values from -6 to 6
Outputs:
- block_out: bfloat16 [12288, 1536], P('dp')
- grad_hidden: float32 [12288, 1536], P('dp')
- grad_norm_gain: float32 [1536], replicated
- grad_gate_weight: float32 [1536, 3072], P(None, 'tensor')
- grad_input_weight: float32 [1536, 3072], P(None, 'tensor')
- grad_step_weight: float32 [1536, 48], P(None, 'tensor')
- grad_state_weight: float32 [1536, 256], replicated
- grad_conv_weight: float32 [4, 3072], P(None, 'tensor')
- grad_state_conv_weight: float32 [4, 256], replicated
- grad_conv_bias: float32 [3072], P('tensor')
- grad_state_conv_bias: float32 [256], replicated
- grad_step_bias: float32 [48], P('tensor')
- grad_decay_log: float32 [48], P('tensor')
- grad_skip_gain: float32 [48], P('tensor')
- grad_gate_norm_gain: float32 [3072], P('tensor')
- grad_out_weight: float32 [3072, 1536], P('tensor')
Inputs may be any that keep to these rules, and one draw needn't show every extreme that they name: `segment_ids`: each value is -1 for an empty slot or the global index of the first slot of its sequence; a sequence lies within the 1536 slots of one dp index, its slots are consecutive; the empty slots of a dp index come after all its sequences and number a multiple of 256; the last dp index has no empty slot, and the last slot of all starts a sequence of one token.
All inputs are finite; a program needn't handle non-finite values.
Results may differ from a plain program's by a relative error of at most 0.0096.
Values may be sent and summed in bfloat16 or wider, within the bound.
No kernel may reach another device: no remote copies, remote signals or barrier semaphores. Data moves between devices by JAX's collectives and lax.ppermute only.
A program may use at most 256 MiB of HBM per device.

v0:
```python
from functools import partial
import jax
import jax.numpy as jnp
from jax import lax
from jax.sharding import PartitionSpec as P

INNER = 3072
GROUP = 256
EPS = 1e-05
HIGH = lax.Precision.HIGHEST


def conv_silu(inputs, weights, biases, segments):
    summed = biases[None, :] + weights[0][None, :] * inputs
    for offset in range(1, weights.shape[0]):
        shifted = jnp.concatenate(
            [jnp.zeros((offset, inputs.shape[1]), inputs.dtype), inputs[:-offset]], axis=0
        )
        seg_shift = jnp.concatenate([jnp.full((offset,), -2, jnp.int32), segments[:-offset]])
        keeping = (seg_shift == segments).astype(inputs.dtype)
        summed = summed + weights[offset][None, :] * shifted * keeping[:, None]
    return jax.nn.silu(summed)


def ssd_scan(values, states, step_raw, step_bias, decay_log, skip_gain, segments, group):
    length = values.shape[0]
    heads = step_bias.shape[0]
    width = values.shape[1] // heads
    state = states.shape[1] // 2
    blocks = length // group
    step = jax.nn.softplus(step_raw + step_bias[None, :])
    rate = step * (-jnp.exp(decay_log))[None, :]
    x_blk = values.reshape(blocks, group, heads, width)
    b_blk = states[:, :state].reshape(blocks, group, state)
    c_blk = states[:, state:].reshape(blocks, group, state)
    step_h = step.reshape(blocks, group, heads).transpose(0, 2, 1)
    cum_h = jnp.cumsum(rate.reshape(blocks, group, heads), axis=1).transpose(0, 2, 1)
    seg_blk = segments.reshape(blocks, group)
    causal = jnp.tril(jnp.ones((group, group), bool))
    same = ((seg_blk[:, :, None] == seg_blk[:, None, :]) & causal[None])[:, None]
    differ = cum_h[:, :, :, None] - cum_h[:, :, None, :]
    decay = jnp.where(same, jnp.exp(jnp.where(same, differ, 0.0)), 0.0)
    inner_cb = jnp.einsum("cin,cjn->cij", c_blk, b_blk, precision=HIGH)
    mixing = decay * inner_cb[:, None] * step_h[:, :, None, :]
    y_diag = jnp.einsum("chij,cjhp->cihp", mixing, x_blk, precision=HIGH)
    last_seg = seg_blk[:, -1]
    to_end = jnp.exp(cum_h[:, :, -1:] - cum_h) * step_h * (seg_blk == last_seg[:, None])[:, None, :]
    weighted = to_end.transpose(0, 2, 1)[..., None] * x_blk
    local_state = jnp.einsum("cjn,cjhp->chnp", b_blk, weighted, precision=HIGH)
    prev_seg = jnp.concatenate([jnp.full((1,), -3, jnp.int32), last_seg[:-1]])
    carry_keep = (last_seg == prev_seg).astype(values.dtype)[:, None] * jnp.exp(cum_h[:, :, -1])

    def advance(entering, pieces):
        local_part, factor = pieces
        return (local_part + factor[:, None, None] * entering, entering)

    start_state = jnp.zeros((heads, state, width), values.dtype)
    _, entering_all = lax.scan(advance, start_state, (local_state, carry_keep))
    reach = jnp.exp(cum_h).transpose(0, 2, 1) * (seg_blk == prev_seg[:, None])[..., None]
    y_off = jnp.einsum("cin,chnp->cihp", c_blk, entering_all, precision=HIGH) * reach[..., None]
    result = y_diag + y_off + skip_gain[None, None, :, None] * x_blk
    return result.reshape(length, heads * width)


def cross_dot(left, right):
    return lax.dot_general(
        left, right, (((0,), (0,)), ((), ())), preferred_element_type=jnp.float32
    )


def back_dot(left, right):
    return lax.dot_general(
        left, right, (((1,), (1,)), ((), ())), preferred_element_type=jnp.float32
    )


def body(
    hidden,
    segment_ids,
    norm_gain,
    gate_weight,
    input_weight,
    step_weight,
    state_weight,
    conv_weight,
    state_conv_weight,
    conv_bias,
    state_conv_bias,
    step_bias,
    decay_log,
    skip_gain,
    gate_norm_gain,
    out_weight,
    cotangent,
):
    valid = (segment_ids >= 0).astype(jnp.float32)[:, None]
    hidden_f = hidden.astype(jnp.float32)
    inverse = lax.rsqrt(jnp.mean(hidden_f * hidden_f, axis=1, keepdims=True) + EPS)
    normed = (hidden_f * inverse * norm_gain[None, :]).astype(jnp.bfloat16)
    gate_pre = jnp.dot(normed, gate_weight, preferred_element_type=jnp.float32)
    input_pre = jnp.dot(normed, input_weight, preferred_element_type=jnp.float32)
    step_pre = jnp.dot(normed, step_weight, preferred_element_type=jnp.float32)
    state_pre = jnp.dot(normed, state_weight, preferred_element_type=jnp.float32)
    conv_out, conv_back = jax.vjp(
        partial(conv_silu, segments=segment_ids), input_pre, conv_weight, conv_bias
    )
    state_out, state_back = jax.vjp(
        partial(conv_silu, segments=segment_ids), state_pre, state_conv_weight, state_conv_bias
    )
    values_f = lax.optimization_barrier(conv_out.astype(jnp.bfloat16)).astype(jnp.float32)
    states_f = lax.optimization_barrier(state_out.astype(jnp.bfloat16)).astype(jnp.float32)
    mixed_y, ssd_back = jax.vjp(
        partial(ssd_scan, segments=segment_ids, group=GROUP),
        values_f,
        states_f,
        step_pre,
        step_bias,
        decay_log,
        skip_gain,
    )
    gate_act = jax.nn.silu(gate_pre)
    gated = mixed_y * gate_act
    square_sum = lax.psum(jnp.sum(gated * gated, axis=1), "tensor")
    gate_inverse = lax.rsqrt(square_sum / INNER + EPS)[:, None]
    gnormed = (gated * gate_inverse * gate_norm_gain[None, :]).astype(jnp.bfloat16)
    partial_mix = jnp.dot(gnormed, out_weight, preferred_element_type=jnp.float32)
    mix = lax.psum(partial_mix, "tensor")
    block_out = (hidden_f + valid * mix).astype(jnp.bfloat16)
    dmix = (cotangent.astype(jnp.float32) * valid).astype(jnp.bfloat16)
    grad_out = cross_dot(gnormed, dmix)
    d_gn = back_dot(dmix, out_weight)
    grad_gnorm = jnp.sum(d_gn * gated * gate_inverse, axis=0)
    scaled = d_gn * gate_norm_gain[None, :]
    dot_sum = lax.psum(jnp.sum(gated * scaled, axis=1), "tensor")
    d_gated = gate_inverse * scaled - gated * gate_inverse**3 * (dot_sum / INNER)[:, None]
    d_y = d_gated * gate_act
    sigma = jax.nn.sigmoid(gate_pre)
    d_gate = d_gated * mixed_y * sigma * (1.0 + gate_pre * (1.0 - sigma))
    d_values, d_states, d_step, grad_sbias, grad_decay, grad_skip = ssd_back(d_y)
    d_input, grad_conv, grad_cbias = conv_back(d_values)
    gate_b = d_gate.astype(jnp.bfloat16)
    input_b = d_input.astype(jnp.bfloat16)
    step_b = d_step.astype(jnp.bfloat16)
    local_back = (
        back_dot(gate_b, gate_weight)
        + back_dot(input_b, input_weight)
        + back_dot(step_b, step_weight)
    )
    summed_back, states_full = lax.psum((local_back, d_states), "tensor")
    d_state_pre, grad_sconv, grad_scbias = state_back(states_full)
    state_b = d_state_pre.astype(jnp.bfloat16)
    d_normed = summed_back + back_dot(state_b, state_weight)
    grad_norm = jnp.sum(d_normed * hidden_f * inverse, axis=0)
    scaled_in = d_normed * norm_gain[None, :]
    grad_hidden = (
        cotangent.astype(jnp.float32)
        + inverse * scaled_in
        - hidden_f * inverse**3 * jnp.mean(hidden_f * scaled_in, axis=1, keepdims=True)
    )
    grad_gate = cross_dot(normed, gate_b)
    grad_input = cross_dot(normed, input_b)
    grad_step = cross_dot(normed, step_b)
    grad_state = cross_dot(normed, state_b)
    summed = lax.psum(
        (
            grad_norm,
            grad_gate,
            grad_input,
            grad_step,
            grad_state,
            grad_conv,
            grad_sconv,
            grad_cbias,
            grad_scbias,
            grad_sbias,
            grad_decay,
            grad_skip,
            grad_gnorm,
            grad_out,
        ),
        "dp",
    )
    (
        grad_norm,
        grad_gate,
        grad_input,
        grad_step,
        grad_state,
        grad_conv,
        grad_sconv,
        grad_cbias,
        grad_scbias,
        grad_sbias,
        grad_decay,
        grad_skip,
        grad_gnorm,
        grad_out,
    ) = summed
    return (
        block_out,
        grad_hidden,
        grad_norm,
        grad_gate,
        grad_input,
        grad_step,
        grad_state,
        grad_conv,
        grad_sconv,
        grad_cbias,
        grad_scbias,
        grad_sbias,
        grad_decay,
        grad_skip,
        grad_gnorm,
        grad_out,
    )


def solution(mesh):
    return jax.shard_map(
        body,
        mesh=mesh,
        in_specs=(
            P("dp", None),
            P("dp"),
            P(),
            P(None, "tensor"),
            P(None, "tensor"),
            P(None, "tensor"),
            P(),
            P(None, "tensor"),
            P(),
            P("tensor"),
            P(),
            P("tensor"),
            P("tensor"),
            P("tensor"),
            P("tensor"),
            P("tensor", None),
            P("dp", None),
        ),
        out_specs=(
            P("dp", None),
            P("dp", None),
            P(),
            P(None, "tensor"),
            P(None, "tensor"),
            P(None, "tensor"),
            P(),
            P(None, "tensor"),
            P(),
            P("tensor"),
            P(),
            P("tensor"),
            P("tensor"),
            P("tensor"),
            P("tensor"),
            P("tensor", None),
        ),
        check_vma=False,
    )
```

profile of v0, /device:TPU:0, one launch (start us, length us, event | category | flops | bytes accessed | tf_op | source)
XLA Modules:
  0.0 1345.6 jit_solution(4326663023551138808)
XLA Ops:
  51.8 9.9 copy.178
  78.2 42.7 %while.34 = (s32[]{:T(128)}, f32[12,128,64]{2,1,0:T(8,128)}, f32[6,12,128,64]{3,2,1,0:T(8,128)}, f32[6,12,1,1]{1,3,2,0:T(1,128)}, f32[6,12,128,64]{2,3,1,0:T(8,128)}, /*index=5*/f32[6,12]{1,0:T(8,128)}, s32[]{:T(128)}, s32[]{:T(128)}) while((s32[]{:T(128)}, f32[12,128,64]{2,1,0:T(8,128)}, f32[6,12,128,64]{3,2,1,0:T(8,128)}, ...), condition=%wide.region_4.5_spmd.clone, body=%wide.region_3.4_spmd.clone.sunk | while | flops 393219 | bytes 4327672 | solution.py:58
  142.3 18.5 %fusion.40 = f32[6,256,12,64]{1,3,2,0:T(8,128)} fusion(f32[6,256,12,64]{1,3,2,0:T(8,128)} %copy.178, f32[6,256,12,64]{1,3,2,0:T(8,128)} %bitcast.225, f32[12]{0:T(128)S(1)} %copy-done.91, f32[6,256,12]{1,2,0:T(8,128)S(1)} %copy-done.30, bf16[6,256,12,64]{1,3,2,0:T(8,128)(2,1)} %copy.176, f32[6,12,256]{2,1,0:T(8,128)S(1)} %bitcast.258, ...), kind=kOutput, calls=%fused_computation.68 | convolution fusion | flops 3652190208 | bytes 18702384 | tf_op jit(solution)/shard_map/jvp(chij,cjhp->cihp)/dot_general | solution.py:45
  160.7 10.7 copy.219
  171.5 9.9 reshape.328
  181.4 10.2 multiply_reduce_fusion.11
  200.2 11.6 multiply_reduce_fusion.2
  217.9 12.3 multiply_reduce_fusion.3
  243.1 19.8 %fusion.77 = f32[6,256,128]{2,1,0:T(8,128)} fusion(f32[6,12,128,64]{3,2,1,0:T(8,128)} %get-tuple-element.547, f32[6,256,12]{1,2,0:T(8,128)S(1)} %copy-done.30, f32[6,256,12,64]{1,0,3,2:T(8,128)} %reshape.302), kind=kOutput, calls=%fused_computation.129 | convolution fusion | flops 1813118976 | bytes 7938048 | tf_op jit(solution)/shard_map/transpose(jvp(cin,chnp->cihp))/dot_general | solution.py:60
  276.3 45.5 %while.35 = (s32[]{:T(128)}, f32[12,128,64]{2,1,0:T(8,128)}, f32[6,12,128,64]{3,2,1,0:T(8,128)}, f32[6,12]{1,0:T(8,128)}, f32[6,12,128,64]{2,3,1,0:T(8,128)}, /*...) while((s32[]{:T(128)}, f32[12,128,64]{2,1,0:T(8,128)}, ...), condition=%wide.region_12.13_spmd.clone, body=%wide.region_10.12_spmd.clone.sunk | while | flops 589816 | bytes 4719024 | solution.py:58
  321.8 18.7 %fusion.80 = f32[6,256,128]{2,1,0:T(8,128)S(1)} fusion(f32[6,12,128,64]{3,2,1,0:T(8,128)} %get-tuple-element.193, f32[6,256,12,64]{1,3,2,0:T(8,128)} %copy.178, f32[6,256,12]{1,2,0:T(8,128)} %copy-done.28), kind=kOutput, calls=%fused_computation.130 | convolution fusion | flops 1813118976 | bytes 7938048 | tf_op jit(solution)/shard_map/transpose(jvp(cjn,cjhp->chnp))/dot_general | solution.py:49
  340.6 8.7 multiply_reduce_fusion.9
  356.2 23.7 %fusion.11 = (f32[6,12,256]{2,1,0:T(8,128)}, f32[6,12,256]{2,1,0:T(8,128)}, f32[6,12,256]{2,1,0:T(8,128)}, f32[6,256,256]{2,1,0:T(8,128)S(1)}) fusion(f32[6,12,256]{2,1,0:T(8,128)S(1)} %bitcast.259, f32[6,256,256]{2,1,0:T(8,128)S(1)} %copy-done.26, f32[6,12,256]{2,1,0:T(8,128)S(1)} %copy-done.25, pred[6,256,256]{2,1,0:T(8,128)(4,1)S(1)} %copy-done.35, ...), kind=kOutput, calls=%fused_computation.31 | convolution fusion | flops 3694209024 | bytes 10985472 | tf_op jit(solution)/shard_map/transpose(jvp(chij,cjhp->cihp))/dot_general | solution.py:45
  386.4 14.9 %reduce-window.16 = f32[6,12,2,128]{3,1,2,0:T(8,128)S(1)} reduce-window(f32[6,12,2,128]{3,1,2,0:T(8,128)S(1)} %copy.201, f32[]{:T(128)} %constant.111.clone.1), window={size=1x1x1x128 pad=0_0x0_0x0_0x0_127}, to_apply=%region_19.20 | reduce-window | flops 2340864 | bytes 147460 | tf_op jit(solution)/shard_map/reduce-window.2
  401.9 24.5 %bitcast_add_fusion.2 = f32[6,256,12,64]{1,3,2,0:T(8,128)} fusion(f32[6,256,12,64]{1,3,2,0:T(8,128)} %get-tuple-element.428, f32[12]{0:T(128)} %param.34, f32[6,256,12]{1,2,0:T(8,128)S(1)} %copy-done.29, f32[6,12,256]{2,1,0:T(8,128)} %bitcast.257, f32[6,256,256]{2,1,0:T(8,128)} %fusion.119, f32[6,12,256]{2,1,0:T(8,128)S(1)} %copy-done.25, ...), kind=kOutput, calls=%fused_computation.62 | convolution fusion | flops 3652190208 | bytes 21061680 | tf_op jit(solution)/shard_map/transpose(jvp(chij,cjhp->cihp))/dot_general | solution.py:45
  426.4 10.7 copy.221
  437.2 10.0 reshape.329
  447.2 9.5 multiply_reduce_fusion.7
  486.8 9.4 fusion.124
  511.6 318.8 %all-reduce.34.cloned.1.call-done = (f32[1536,1536]{1,0:T(8,128)}, f32[1536,1536]{1,0:T(8,128)}, f32[1536,256]{1,0:T(8,128)}) async-done(((f32[1536,1536]{1,0:T(8,128)}, f32[1536,1536]{1,0:T(8,128)}, f32[1536,256]{1,0:T(8,128)}), (f32[1536,1536]{1,0:T(8,128)}, f32[1536,1536]{1,0:T(8,128)}, f32[1536,256]{1,0:T(8,128)})) %all-reduce.34.cloned.1.call-update) | async-done | bytes 20447248 | tf_op jit(solution)/shard_map/psum | solution.py:127
  841.0 9.4 fusion.21
  850.4 40.7 %all-reduce.26 = (f32[1536]{0:T(1024)}, f32[4,768]{1,0:T(4,128)}, f32[4,256]{1,0:T(4,128)}, f32[768]{0:T(1024)}, f32[256]{0:T(256)}, /*index=5*/f32[12]{0:T(128)}, f32[12]{0:T(128)}, f32[12]{0:T(128)}, f32[768]{0:T(1024)}) all-reduce(f32[1536]{0:T(1024)S(1)} %get-tuple-element.309, ...), channel_id=1, replica_groups=mesh['dp'=8,'tensor'=4] {'dp'}, use_global_device_ids=true, to_apply=%region_26.27 | all-reduce | flops 7460 | bytes 59680 | tf_op jit(solution)/shard_map/psum | solution.py:164
  891.1 17.0 %fusion.13 = (f32[1536,1536]{1,0:T(8,128)}, bf16[1536,1536]{1,0:T(8,128)(2,1)}) fusion(bf16[1536,1536]{1,0:T(8,128)(2,1)} %param.37, bf16[1536,1536]{1,0:T(8,128)(2,1)} %param.21, f32[1536,1536]{1,0:T(8,128)} %get-tuple-element.429, f32[1536]{0:T(1024)S(1)} %broadcast_multiply_fusion.8, f32[1536]{0:T(1024)S(1)} %copy-done.68, f32[1536]{0:T(1024)S(1)} %copy-done.55, ...), kind=kLoop, calls=%fused_computation.35 | loop fusion | flops 25952256 | bytes 42498048 | tf_op jit(solution)/shard_map/sub | solution.py:156
  908.1 418.2 %all-reduce.32.cloned.1.call-done = (f32[1536,768]{1,0:T(8,128)}, f32[1536,768]{1,0:T(8,128)}, f32[1536,12]{0,1:T(8,128)}, f32[1536,256]{1,0:T(8,128)}, f32[768,1536]{1,0:T(8,128)}) async-done(((f32[1536,768]{1,0:T(8,128)}, f32[1536,768]{1,0:T(8,128)}, f32[1536,12]{0,1:T(8,128)}, f32[1536,256]{1,0:T(8,128)}, f32[768,1536]{1,0:T(8,128)}), (f32[1536,768]{1,0:T(8,128)}, f32[1536,768]{1,0:T(8,128)}, ...) | async-done | bytes 15802384 | tf_op jit(solution)/shard_map/psum | solution.py:164
  (424 shorter events, 292.6 us)
Async XLA Ops:
  7.2 174.3 %copy-start = (bf16[1536,768]{1,0:T(8,128)(2,1)S(1)}, bf16[1536,768]{1,0:T(8,128)(2,1)}, u32[]{:S(2)}) copy-start(bf16[1536,768]{1,0:T(8,128)(2,1)} %param.24) | copy-start | bytes 7077892
  7.2 823.2 %all-reduce.34.cloned.1.call-start = ((), (), s32[]{:S(2)}) async-start(), calls=%async_computation.1 | async-start | bytes 40894464 | tf_op jit(solution)/shard_map/psum | solution.py:127
  19.1 46.5 %copy-start.37 = (f32[1536]{0:T(1024)}, f32[1536]{0:T(1024)S(1)}, u32[]{:S(2)}) copy-start(f32[1536]{0:T(1024)S(1)} %get-tuple-element.415) | copy-start | bytes 18436
  19.1 46.5 %copy-start.39 = (f32[1536]{0:T(1024)}, f32[1536]{0:T(1024)S(1)}, u32[]{:S(2)}) copy-start(f32[1536]{0:T(1024)S(1)} %get-tuple-element.413) | copy-start | bytes 18436
  19.1 46.5 %copy-start.41 = (f32[1536]{0:T(1024)}, f32[1536]{0:T(1024)S(1)}, u32[]{:S(2)}) copy-start(f32[1536]{0:T(1024)S(1)} %get-tuple-element.414) | copy-start | bytes 18436
  51.6 19.3 %copy-start.23 = (f32[6,12,256]{2,1,0:T(8,128)}, f32[6,12,256]{2,1,0:T(8,128)S(1)}, u32[]{:S(2)}) copy-start(f32[6,12,256]{2,1,0:T(8,128)S(1)} %reduce_window_sum.39) | copy-start | bytes 221188
  51.8 19.1 %copy-start.17 = (f32[6,256,12]{1,0,2:T(8,128)}, f32[6,256,12]{1,0,2:T(8,128)S(1)}, u32[]{:S(2)}) copy-start(f32[6,256,12]{1,0,2:T(8,128)S(1)} %reshape.299) | copy-start | bytes 221188
  181.4 18.8 %copy-start.44 = (f32[768]{0:T(1024)S(1)}, f32[768]{0:T(1024)}, u32[]{:S(2)}) copy-start(f32[768]{0:T(1024)} %param.35) | copy-start | bytes 9220
  181.4 18.8 %copy-start.56 = (f32[1536]{0:T(1024)S(1)}, f32[1536]{0:T(1024)}, u32[]{:S(2)}) copy-start(f32[1536]{0:T(1024)} %get-tuple-element.412) | copy-start | bytes 18436
  243.1 19.8 %copy-start.4 = (f32[6,256,12,64]{1,0,3,2:T(8,128)S(1)}, f32[6,256,12,64]{1,0,3,2:T(8,128)}, u32[]{:S(2)}) copy-start(f32[6,256,12,64]{1,0,3,2:T(8,128)} %reshape.302) | copy-start | bytes 14155780
  321.8 18.7 %copy-start.7 = (f32[6,12,128,64]{3,2,1,0:T(8,128)S(1)}, f32[6,12,128,64]{3,2,1,0:T(8,128)}, u32[]{:S(2)}) copy-start(f32[6,12,128,64]{3,2,1,0:T(8,128)} %get-tuple-element.193) | copy-start | bytes 7077892
  321.8 18.7 %copy-start.12 = (bf16[1536,128]{1,0:T(8,128)(2,1)S(1)}, bf16[1536,128]{1,0:T(8,128)(2,1)}, u32[]{:S(2)}) copy-start(bf16[1536,128]{1,0:T(8,128)(2,1)} %copy-done.10) | copy-start | bytes 1179652
  321.8 27.5 %slice-start.12 = ((s8[4718592]{0:T(1024)(128)(4,1)}), s8[4194304]{0:T(1024)(128)(4,1)S(1)}, s32[]{:S(2)}) async-start(s8[4718592]{0:T(1024)(128)(4,1)} %bitcast.229), calls=%async_computation.14 | async-start | bytes 8388608
  340.6 15.6 %slice-start.2 = ((s8[6291456]{0:T(1024)(128)(4,1)}), s8[4194304]{0:T(1024)(128)(4,1)S(1)}, s32[]{:S(2)}) async-start(s8[6291456]{0:T(1024)(128)(4,1)} %bitcast.216), calls=%async_computation.4 | async-start | bytes 8388608
  356.2 23.7 %copy-start.14 = (f32[6,256,128]{2,1,0:T(8,128)S(1)}, f32[6,256,128]{2,1,0:T(8,128)}, u32[]{:S(2)}) copy-start(f32[6,256,128]{2,1,0:T(8,128)} %fusion.77) | copy-start | bytes 2359300
  356.2 25.5 %copy-start.9 = (bf16[1536,128]{1,0:T(8,128)(2,1)S(1)}, bf16[1536,128]{1,0:T(8,128)(2,1)}, u32[]{:S(2)}) copy-start(bf16[1536,128]{1,0:T(8,128)(2,1)} %get-tuple-element.400) | copy-start | bytes 1179652
  380.0 22.0 %copy-start.29 = (f32[6,256,12]{1,2,0:T(8,128)S(1)}, f32[6,256,12]{1,2,0:T(8,128)}, u32[]{:S(2)}) copy-start(f32[6,256,12]{1,2,0:T(8,128)} %copy-done.28) | copy-start | bytes 221188
  437.2 10.0 copy-start.38
  437.2 19.6 %slice-start = ((s8[4718592]{0:T(1024)(128)(4,1)}), s8[524288]{0:T(1024)(128)(4,1)S(1)}, s32[]{:S(2)}) async-start(s8[4718592]{0:T(1024)(128)(4,1)} %bitcast.205), calls=%async_computation.2 | async-start | bytes 1048576
  482.6 843.6 %all-reduce.32.cloned.1.call-start = ((), (), s32[]{:S(2)}) async-start(), calls=%async_computation | async-start | bytes 31653888 | tf_op jit(solution)/shard_map/psum | solution.py:164
  486.8 18.1 %slice-start.8 = ((s8[4718592]{0:T(1024)(128)(4,1)}), s8[4194304]{0:T(1024)(128)(4,1)S(1)}, s32[]{:S(2)}) async-start(s8[4718592]{0:T(1024)(128)(4,1)} %bitcast.223), calls=%async_computation.10 | async-start | bytes 8388608
  486.8 18.1 %slice-start.14 = ((s8[4718592]{0:T(1024)(128)(4,1)}), s8[4194304]{0:T(1024)(128)(4,1)S(1)}, s32[]{:S(2)}) async-start(s8[4718592]{0:T(1024)(128)(4,1)} %bitcast.231), calls=%async_computation.16 | async-start | bytes 8388608
  841.0 50.1 %copy-start.68 = (f32[1536]{0:T(1024)S(1)}, f32[1536]{0:T(1024)}, u32[]{:S(2)}) copy-start(f32[1536]{0:T(1024)} %get-tuple-element.408) | copy-start | bytes 18436
  1326.3 10.0 slice-start.16
  (90 other events, 471.8 us)
Sparse Core Ops, SparseCore 0:
  482.8 347.5 all-reduce.33
  840.2 486.0 all-reduce.31
where the time goes:
time: 1350 us
  waiting for transfers between devices  737 us (55%)
  matrix products  231 us (17%)
  local copies, waits for them, and re-layouts  161 us (12%)
  other arithmetic  145 us (11%)
  blocking collectives  55.2 us (4%)
  between operations  15.8 us (1%)
    psum x1, waiting for transfers between devices, body(): lax.psum((grad_norm, grad_gate, grad_input, grad_step, grad_state, grad_c...  418 us
    psum x1, waiting for transfers between devices, body(): mix = lax.psum(partial_mix, 'tensor')  319 us
    dot_general x3, matrix products, ssd_scan(): y_diag = jnp.einsum('chij,cjhp->cihp', mixing, x_blk, precision=HIGH)  66.6 us
    reshape x6, local copies, waits for them, and re-layouts, ssd_scan(): x_blk = values.reshape(blocks, group, heads, width)  54.7 us
    psum x1, blocking collectives, body(): lax.psum((grad_norm, grad_gate, grad_input, grad_step, grad_state, grad_c...  40.7 us
    dot_general x5, matrix products, back_dot(): lax.dot_general(left, right, (((1,), (1,)), ((), ())), preferred_element_...  36.6 us
    dot_general x3, matrix products, ssd_scan(): local_state = jnp.einsum('cjn,cjhp->chnp', b_blk, weighted, precision=HIGH)  31.2 us
    dot_general x5, matrix products, cross_dot(): lax.dot_general(left, right, (((0,), (0,)), ((), ())), preferred_element_...  31.2 us
  transfers between devices with their start and end apart: 2, of which 2 were waited for; matrix products, arithmetic and copies ran while one was open for 4% of the time, Pallas kernels for 0%

commit v1 on v0

--- a/solution.py
+++ b/solution.py
@@ -124,7 +124,9 @@
     gate_inverse = lax.rsqrt(square_sum / INNER + EPS)[:, None]
     gnormed = (gated * gate_inverse * gate_norm_gain[None, :]).astype(jnp.bfloat16)
     partial_mix = jnp.dot(gnormed, out_weight, preferred_element_type=jnp.float32)
-    mix = lax.psum(partial_mix, "tensor")
+    mix = partial_mix
+    for hop in (1, 2):
+        mix = mix + lax.ppermute(mix, "tensor", [(dev, dev ^ hop) for dev in range(4)])
     block_out = (hidden_f + valid * mix).astype(jnp.bfloat16)
     dmix = (cotangent.astype(jnp.float32) * valid).astype(jnp.bfloat16)
     grad_out = cross_dot(gnormed, dmix)

time: 1350 us -> 1200 us (0.89)
  waiting for transfers between devices: 737 us -> 563 us
  other arithmetic: 145 us -> 160 us
    psum x1, waiting for transfers between devices: 418 us -> 250 us  [body(): lax.psum((grad_norm, grad_gate, grad_input, grad_step, grad_state, grad_c...]
    psum x1, waiting for transfers between devices: 319 us -> 160 us  [body(): summed_back, states_full = lax.psum((local_back, d_states), 'tensor')]
    ppermute x0 -> x2, waiting for transfers between devices: none -> 154 us  [body(): lax.ppermute(mix, 'tensor', [(dev, dev ^ hop) for dev in range(4)])]
  transfers between devices with their start and end apart: 2 -> 4, of which waited for: 2 -> 3; matrix products, arithmetic and copies ran while one was open for 4% -> 7% of each run, Pallas kernels for 0% -> 0%
where the time goes in v1:
time: 1200 us; the launch traced here: 1190 us
  waiting for transfers between devices  563 us (47%)
  matrix products  231 us (19%)
  local copies, waits for them, and re-layouts  161 us (13%)
  other arithmetic  160 us (13%)
  blocking collectives  55.6 us (5%)
  between operations  15.7 us (1%)
    psum x1, waiting for transfers between devices, body(): lax.psum((grad_norm, grad_gate, grad_input, grad_step, grad_state, grad_c...  250 us
    psum x1, waiting for transfers between devices, body(): summed_back, states_full = lax.psum((local_back, d_states), 'tensor')  160 us
    ppermute x2, waiting for transfers between devices, body(): lax.ppermute(mix, 'tensor', [(dev, dev ^ hop) for dev in range(4)])  154 us
    dot_general x3, matrix products, ssd_scan(): y_diag = jnp.einsum('chij,cjhp->cihp', mixing, x_blk, precision=HIGH)  66.7 us
    reshape x6, local copies, waits for them, and re-layouts, ssd_scan(): x_blk = values.reshape(blocks, group, heads, width)  54.7 us
    psum x1, blocking collectives, body(): lax.psum((grad_norm, grad_gate, grad_input, grad_step, grad_state, grad_c...  41 us
    dot_general x5, matrix products, back_dot(): lax.dot_general(left, right, (((1,), (1,)), ((), ())), preferred_element_...  36.4 us
    dot_general x3, matrix products, ssd_scan(): local_state = jnp.einsum('cjn,cjhp->chnp', b_blk, weighted, precision=HIGH)  31.2 us
  transfers between devices with their start and end apart: 4, of which 3 were waited for; matrix products, arithmetic and copies ran while one was open for 7% of the time, Pallas kernels for 0%

profile of v1, /device:TPU:0, one launch (start us, length us, event | category | flops | bytes accessed | tf_op | source)
XLA Modules:
  0.0 1187.1 jit_solution(14132665228210814893)
XLA Ops:
  51.8 9.9 copy.178
  78.2 42.8 %while.34 = (s32[]{:T(128)}, f32[12,128,64]{2,1,0:T(8,128)}, f32[6,12,128,64]{3,2,1,0:T(8,128)}, f32[6,12,1,1]{1,3,2,0:T(1,128)}, f32[6,12,128,64]{2,3,1,0:T(8,128)}, /*index=5*/f32[6,12]{1,0:T(8,128)}, s32[]{:T(128)}, s32[]{:T(128)}) while((s32[]{:T(128)}, f32[12,128,64]{2,1,0:T(8,128)}, f32[6,12,128,64]{3,2,1,0:T(8,128)}, ...), condition=%wide.region_4.5_spmd.clone, body=%wide.region_3.4_spmd.clone.sunk | while | flops 393219 | bytes 4327672 | solution.py:58
  142.3 18.5 %fusion.40 = f32[6,256,12,64]{1,3,2,0:T(8,128)} fusion(f32[6,256,12,64]{1,3,2,0:T(8,128)} %copy.178, f32[6,256,12,64]{1,3,2,0:T(8,128)} %bitcast.227, f32[12]{0:T(128)S(1)} %copy-done.90, f32[6,256,12]{1,2,0:T(8,128)S(1)} %copy-done.30, bf16[6,256,12,64]{1,3,2,0:T(8,128)(2,1)} %copy.176, f32[6,12,256]{2,1,0:T(8,128)S(1)} %bitcast.258, ...), kind=kOutput, calls=%fused_computation.68 | convolution fusion | flops 3652190208 | bytes 18702384 | tf_op jit(solution)/shard_map/jvp(chij,cjhp->cihp)/dot_general | solution.py:45
  160.8 10.7 copy.219
  171.5 9.9 reshape.328
  181.5 10.3 multiply_reduce_fusion.11
  200.3 11.5 multiply_reduce_fusion.2
  217.9 12.2 %multiply_reduce_fusion.3 = (f32[768]{0:T(1024)}, f32[1536,768]{1,0:T(8,128)}, bf16[1536,768]{1,0:T(8,128)(2,1)}) fusion(bf16[1536,768]{1,0:T(8,128)(2,1)} %get-tuple-element.385, f32[1536,768]{1,0:T(8,128)} %get-tuple-element.424, f32[1536]{0:T(1024)S(1)} %broadcast_multiply_fusion.7, f32[1536,768]{1,0:T(8,128)} %get-tuple-element.382, ...), kind=kLoop, calls=%fused_computation.70 | loop fusion | flops 23592192 | bytes 28336128 | tf_op jit(solution)/shard_map/transpose(jvp())/reduce_sum | solution.py:61
  243.2 19.8 %fusion.77 = f32[6,256,128]{2,1,0:T(8,128)} fusion(f32[6,12,128,64]{3,2,1,0:T(8,128)} %get-tuple-element.546, f32[6,256,12]{1,2,0:T(8,128)S(1)} %copy-done.30, f32[6,256,12,64]{1,0,3,2:T(8,128)} %reshape.302), kind=kOutput, calls=%fused_computation.129 | convolution fusion | flops 1813118976 | bytes 7938048 | tf_op jit(solution)/shard_map/transpose(jvp(cin,chnp->cihp))/dot_general | solution.py:60
  276.3 45.6 %while.35 = (s32[]{:T(128)}, f32[12,128,64]{2,1,0:T(8,128)}, f32[6,12,128,64]{3,2,1,0:T(8,128)}, f32[6,12]{1,0:T(8,128)}, f32[6,12,128,64]{2,3,1,0:T(8,128)}, /*...) while((s32[]{:T(128)}, f32[12,128,64]{2,1,0:T(8,128)}, ...), condition=%wide.region_11.12_spmd.clone, body=%wide.region_9.11_spmd.clone.sunk | while | flops 589816 | bytes 4719024 | solution.py:58
  321.9 18.6 %fusion.80 = f32[6,256,128]{2,1,0:T(8,128)S(1)} fusion(f32[6,12,128,64]{3,2,1,0:T(8,128)} %get-tuple-element.193, f32[6,256,12,64]{1,3,2,0:T(8,128)} %copy.178, f32[6,256,12]{1,2,0:T(8,128)} %copy-done.28), kind=kOutput, calls=%fused_computation.130 | convolution fusion | flops 1813118976 | bytes 7938048 | tf_op jit(solution)/shard_map/transpose(jvp(cjn,cjhp->chnp))/dot_general | solution.py:49
  349.5 24.1 %fusion.11 = (f32[6,12,256]{2,1,0:T(8,128)}, f32[6,12,256]{2,1,0:T(8,128)}, f32[6,12,256]{2,1,0:T(8,128)}, f32[6,256,256]{2,1,0:T(8,128)S(1)}) fusion(f32[6,12,256]{2,1,0:T(8,128)S(1)} %bitcast.259, f32[6,256,256]{2,1,0:T(8,128)S(1)} %copy-done.26, f32[6,12,256]{2,1,0:T(8,128)S(1)} %copy-done.25, pred[6,256,256]{2,1,0:T(8,128)(4,1)S(1)} %copy-done.35, ...), kind=kOutput, calls=%fused_computation.31 | convolution fusion | flops 3694209024 | bytes 10985472 | tf_op jit(solution)/shard_map/transpose(jvp(chij,cjhp->cihp))/dot_general | solution.py:45
  380.1 14.9 %reduce-window.16 = f32[6,12,2,128]{3,1,2,0:T(8,128)S(1)} reduce-window(f32[6,12,2,128]{3,1,2,0:T(8,128)S(1)} %copy.201, f32[]{:T(128)} %constant.111.clone.1), window={size=1x1x1x128 pad=0_0x0_0x0_0x0_127}, to_apply=%region_18.19 | reduce-window | flops 2340864 | bytes 147460 | tf_op jit(solution)/shard_map/reduce-window.2
  395.6 24.2 %bitcast_add_fusion.2 = f32[6,256,12,64]{1,3,2,0:T(8,128)} fusion(f32[6,256,12,64]{1,3,2,0:T(8,128)} %get-tuple-element.427, f32[12]{0:T(128)} %param.34, f32[6,256,12]{1,2,0:T(8,128)S(1)} %copy-done.29, f32[6,12,256]{2,1,0:T(8,128)} %bitcast.257, f32[6,256,256]{2,1,0:T(8,128)} %fusion.119, f32[6,12,256]{2,1,0:T(8,128)S(1)} %copy-done.25, ...), kind=kOutput, calls=%fused_computation.62 | convolution fusion | flops 3652190208 | bytes 21061680 | tf_op jit(solution)/shard_map/transpose(jvp(chij,cjhp->cihp))/dot_general | solution.py:45
  419.8 10.7 copy.221
  430.5 10.0 reshape.329
  440.5 9.7 multiply_reduce_fusion.7
  476.3 10.8 fusion.106
  512.2 159.7 %all-reduce.34.cloned.1.call-done = (f32[1536,1536]{1,0:T(8,128)}, f32[1536,256]{1,0:T(8,128)}) async-done(((f32[1536,1536]{1,0:T(8,128)}, f32[1536,256]{1,0:T(8,128)}), (f32[1536,1536]{1,0:T(8,128)}, f32[1536,256]{1,0:T(8,128)})) %all-reduce.34.cloned.1.call-update) | async-done | bytes 11010064 | tf_op jit(solution)/shard_map/psum | solution.py:151
  681.8 12.8 %add.238 = f32[1536,1536]{1,0:T(8,128)} add(f32[1536,1536]{1,0:T(8,128)} %fusion.106, f32[1536,1536]{1,0:T(8,128)} %collective-permute-done) | non-fusion elementwise | flops 2359296 | bytes 28311552 | tf_op jit(solution)/shard_map/add | solution.py:129
  704.1 41.0 %all-reduce.26 = (f32[1536]{0:T(1024)}, f32[4,768]{1,0:T(4,128)}, f32[4,256]{1,0:T(4,128)}, f32[768]{0:T(1024)}, f32[256]{0:T(256)}, /*index=5*/f32[12]{0:T(128)}, f32[12]{0:T(128)}, f32[12]{0:T(128)}, f32[768]{0:T(1024)}) all-reduce(f32[1536]{0:T(1024)S(1)} %get-tuple-element.309, ...), channel_id=1, replica_groups=mesh['dp'=8,'tensor'=4] {'dp'}, use_global_device_ids=true, to_apply=%region_25.26 | all-reduce | flops 7460 | bytes 59680 | tf_op jit(solution)/shard_map/psum | solution.py:166
  745.1 153.5 %collective-permute-done.1 = f32[1536,1536]{1,0:T(8,128)} collective-permute-done((f32[1536,1536]{1,0:T(8,128)}, f32[1536,1536]{1,0:T(8,128)}, u32[]{:S(2)}, u32[]{:S(2)}) %collective-permute-start.1) | collective-permute-done | bytes 9437216 | tf_op jit(solution)/shard_map/ppermute | solution.py:129
  898.6 19.3 %fusion.13 = (f32[1536,1536]{1,0:T(8,128)}, bf16[1536,1536]{1,0:T(8,128)(2,1)}) fusion(bf16[1536,1536]{1,0:T(8,128)(2,1)} %param.37, bf16[1536,1536]{1,0:T(8,128)(2,1)} %param.21, f32[1536,1536]{1,0:T(8,128)} %get-tuple-element.428, f32[1536]{0:T(1024)S(1)} %broadcast_multiply_fusion.8, f32[1536]{0:T(1024)S(1)} %copy-done.68, f32[1536]{0:T(1024)S(1)} %copy-done.55, ...), kind=kLoop, calls=%fused_computation.35 | loop fusion | flops 28311552 | bytes 51935232 | tf_op jit(solution)/shard_map/sub | solution.py:158
  917.9 249.9 %all-reduce.32.cloned.1.call-done = (f32[1536,768]{1,0:T(8,128)}, f32[1536,768]{1,0:T(8,128)}, f32[1536,12]{0,1:T(8,128)}, f32[1536,256]{1,0:T(8,128)}, f32[768,1536]{1,0:T(8,128)}) async-done(((f32[1536,768]{1,0:T(8,128)}, f32[1536,768]{1,0:T(8,128)}, f32[1536,12]{0,1:T(8,128)}, f32[1536,256]{1,0:T(8,128)}, f32[768,1536]{1,0:T(8,128)}), (f32[1536,768]{1,0:T(8,128)}, f32[1536,768]{1,0:T(8,128)}, ...) | async-done | bytes 15802384 | tf_op jit(solution)/shard_map/psum | solution.py:166
  (427 shorter events, 309.0 us)
Async XLA Ops:
  7.2 174.3 %copy-start = (bf16[1536,768]{1,0:T(8,128)(2,1)S(1)}, bf16[1536,768]{1,0:T(8,128)(2,1)}, u32[]{:S(2)}) copy-start(bf16[1536,768]{1,0:T(8,128)(2,1)} %param.24) | copy-start | bytes 7077892
  7.2 664.6 %all-reduce.34.cloned.1.call-start = ((), (), s32[]{:S(2)}) async-start(), calls=%async_computation.1 | async-start | bytes 22020096 | tf_op jit(solution)/shard_map/psum | solution.py:151
  19.0 46.5 %copy-start.37 = (f32[1536]{0:T(1024)}, f32[1536]{0:T(1024)S(1)}, u32[]{:S(2)}) copy-start(f32[1536]{0:T(1024)S(1)} %get-tuple-element.414) | copy-start | bytes 18436
  19.0 46.5 %copy-start.39 = (f32[1536]{0:T(1024)}, f32[1536]{0:T(1024)S(1)}, u32[]{:S(2)}) copy-start(f32[1536]{0:T(1024)S(1)} %get-tuple-element.412) | copy-start | bytes 18436
  19.0 46.5 %copy-start.41 = (f32[1536]{0:T(1024)}, f32[1536]{0:T(1024)S(1)}, u32[]{:S(2)}) copy-start(f32[1536]{0:T(1024)S(1)} %get-tuple-element.413) | copy-start | bytes 18436
  51.6 19.3 %copy-start.23 = (f32[6,12,256]{2,1,0:T(8,128)}, f32[6,12,256]{2,1,0:T(8,128)S(1)}, u32[]{:S(2)}) copy-start(f32[6,12,256]{2,1,0:T(8,128)S(1)} %reduce_window_sum.39) | copy-start | bytes 221188
  51.8 19.1 %copy-start.17 = (f32[6,256,12]{1,0,2:T(8,128)}, f32[6,256,12]{1,0,2:T(8,128)S(1)}, u32[]{:S(2)}) copy-start(f32[6,256,12]{1,0,2:T(8,128)S(1)} %reshape.299) | copy-start | bytes 221188
  181.5 18.8 %copy-start.44 = (f32[768]{0:T(1024)S(1)}, f32[768]{0:T(1024)}, u32[]{:S(2)}) copy-start(f32[768]{0:T(1024)} %param.35) | copy-start | bytes 9220
  181.5 18.9 %copy-start.56 = (f32[1536]{0:T(1024)S(1)}, f32[1536]{0:T(1024)}, u32[]{:S(2)}) copy-start(f32[1536]{0:T(1024)} %get-tuple-element.411) | copy-start | bytes 18436
  243.2 19.8 %copy-start.4 = (f32[6,256,12,64]{1,0,3,2:T(8,128)S(1)}, f32[6,256,12,64]{1,0,3,2:T(8,128)}, u32[]{:S(2)}) copy-start(f32[6,256,12,64]{1,0,3,2:T(8,128)} %reshape.302) | copy-start | bytes 14155780
  321.9 18.6 %copy-start.7 = (f32[6,12,128,64]{3,2,1,0:T(8,128)S(1)}, f32[6,12,128,64]{3,2,1,0:T(8,128)}, u32[]{:S(2)}) copy-start(f32[6,12,128,64]{3,2,1,0:T(8,128)} %get-tuple-element.193) | copy-start | bytes 7077892
  321.9 18.6 %copy-start.12 = (bf16[1536,128]{1,0:T(8,128)(2,1)S(1)}, bf16[1536,128]{1,0:T(8,128)(2,1)}, u32[]{:S(2)}) copy-start(bf16[1536,128]{1,0:T(8,128)(2,1)} %copy-done.10) | copy-start | bytes 1179652
  321.9 27.5 %slice-start.2 = ((s8[6291456]{0:T(1024)(128)(4,1)}), s8[4194304]{0:T(1024)(128)(4,1)S(1)}, s32[]{:S(2)}) async-start(s8[6291456]{0:T(1024)(128)(4,1)} %bitcast.216), calls=%async_computation.4 | async-start | bytes 8388608
  349.5 24.1 %copy-start.14 = (f32[6,256,128]{2,1,0:T(8,128)S(1)}, f32[6,256,128]{2,1,0:T(8,128)}, u32[]{:S(2)}) copy-start(f32[6,256,128]{2,1,0:T(8,128)} %fusion.77) | copy-start | bytes 2359300
  349.5 25.9 %copy-start.9 = (bf16[1536,128]{1,0:T(8,128)(2,1)S(1)}, bf16[1536,128]{1,0:T(8,128)(2,1)}, u32[]{:S(2)}) copy-start(bf16[1536,128]{1,0:T(8,128)(2,1)} %get-tuple-element.399) | copy-start | bytes 1179652
  373.6 22.0 %copy-start.29 = (f32[6,256,12]{1,2,0:T(8,128)S(1)}, f32[6,256,12]{1,2,0:T(8,128)}, u32[]{:S(2)}) copy-start(f32[6,256,12]{1,2,0:T(8,128)} %copy-done.28) | copy-start | bytes 221188
  430.5 19.7 %slice-start = ((s8[4718592]{0:T(1024)(128)(4,1)}), s8[524288]{0:T(1024)(128)(4,1)S(1)}, s32[]{:S(2)}) async-start(s8[4718592]{0:T(1024)(128)(4,1)} %bitcast.205), calls=%async_computation.2 | async-start | bytes 1048576
  476.1 691.8 %all-reduce.32.cloned.1.call-start = ((), (), s32[]{:S(2)}) async-start(), calls=%async_computation | async-start | bytes 31653888 | tf_op jit(solution)/shard_map/psum | solution.py:166
  476.3 23.3 %slice-start.6 = ((s8[4718592]{0:T(1024)(128)(4,1)}), s8[524288]{0:T(1024)(128)(4,1)S(1)}, s32[]{:S(2)}) async-start(s8[4718592]{0:T(1024)(128)(4,1)} %bitcast.221), calls=%async_computation.8 | async-start | bytes 1048576
  487.2 194.6 %collective-permute-start = (f32[1536,1536]{1,0:T(8,128)}, f32[1536,1536]{1,0:T(8,128)}, u32[]{:S(2)}, u32[]{:S(2)}) collective-permute-start(f32[1536,1536]{1,0:T(8,128)} %fusion.106), channel_id=1, source_target_pairs={{0,1},{1,0},{2,3},{3,2},{4,5},{5,4},{6,7},{7,6},{8,9},{9,8},{10,11... | collective-permute-start | bytes 28311560 | tf_op jit(solution)/shard_map/ppermute | solution.py:129
  491.0 14.7 %slice-start.10 = ((s8[4718592]{0:T(1024)(128)(4,1)}), s8[4194304]{0:T(1024)(128)(4,1)S(1)}, s32[]{:S(2)}) async-start(s8[4718592]{0:T(1024)(128)(4,1)} %bitcast.225), calls=%async_computation.12 | async-start | bytes 8388608
  491.0 14.7 %slice-start.14 = ((s8[4718592]{0:T(1024)(128)(4,1)}), s8[4194304]{0:T(1024)(128)(4,1)S(1)}, s32[]{:S(2)}) async-start(s8[4718592]{0:T(1024)(128)(4,1)} %bitcast.231), calls=%async_computation.16 | async-start | bytes 8388608
  694.6 204.0 %collective-permute-start.1 = (f32[1536,1536]{1,0:T(8,128)}, f32[1536,1536]{1,0:T(8,128)}, u32[]{:S(2)}, u32[]{:S(2)}) collective-permute-start(f32[1536,1536]{1,0:T(8,128)} %add.238), channel_id=1, source_target_pairs={{0,2},{1,3},{2,0},{3,1},{4,6},{5,7},{6,4},{7,5},{8,10},{9,11},{10,... | collective-permute-start | bytes 28311560 | tf_op jit(solution)/shard_map/ppermute | solution.py:129
  694.9 203.7 %copy-start.68 = (f32[1536]{0:T(1024)S(1)}, f32[1536]{0:T(1024)}, u32[]{:S(2)}) copy-start(f32[1536]{0:T(1024)} %get-tuple-element.407) | copy-start | bytes 18436
  (91 other events, 550.0 us)
Sparse Core Ops, SparseCore 0:
  476.2 195.6 all-reduce.33
  681.8 485.9 all-reduce.31
